TPU v7x, 32 devices: a whole 2x2x4 slice. The times are simulated.
32 devices in a mesh: expert: 8 (over z, y), tensor: 4 (over x, core).
Axes of the slice: x: 2, y: 2, z: 4, core: 2. Of those that a mesh axis runs over, the one named last changes fastest.
Arguments:
- block_input: bfloat16 [8192, 2048], P('expert', 'tensor'), may hold values from -6 to 6
- cotangent: bfloat16 [8192, 2048], P('expert', 'tensor'), may hold values from -6 to 6
- lengths: int32 [8], P('expert'), may hold values from 256 to 1024, as said below
- routes: int32 [8192, 8], P('expert'), may hold values from 0 to 15, all different within a row; in each aligned block of 1024 rows (0 to 1023, 1024 to 2047, ...) at most 576 rows name the same one
- g_attn: float32 [2048], replicated, may hold values from 0.5 to 1.5
- w_query: bfloat16 [2048, 2048], P(None, 'tensor'), may hold values from -0.125 to 0.125
- w_key: bfloat16 [2048, 2048], P(None, 'tensor'), may hold values from -0.125 to 0.125
- w_value: bfloat16 [2048, 2048], P(None, 'tensor'), may hold values from -0.125 to 0.125
- g_query: float32 [2048], P('tensor'), may hold values from 0.5 to 1.5
- g_key: float32 [2048], P('tensor'), may hold values from 0.5 to 1.5
- w_out: bfloat16 [2048, 2048], P('tensor'), may hold values from -0.5 to 0.5
- g_moe: float32 [2048], replicated, may hold values from 0.5 to 1.5
- w_router: bfloat16 [2048, 16], replicated, may hold values from -0.125 to 0.125
- w_gate: bfloat16 [16, 2048, 1024], P('expert', None, 'tensor'), may hold values from -0.125 to 0.125
- w_up: bfloat16 [16, 2048, 1024], P('expert', None, 'tensor'), may hold values from -0.125 to 0.125
- w_down: bfloat16 [16, 1024, 2048], P('expert', 'tensor'), may hold values from -6 to 6
Outputs:
- output: bfloat16 [8192, 2048], P('expert', 'tensor')
- grad_input: bfloat16 [8192, 2048], P('expert', 'tensor')
- grad_g_attn: float32 [2048], replicated
- grad_w_query: float32 [2048, 2048], P(None, 'tensor')
- grad_w_key: float32 [2048, 2048], P(None, 'tensor')
- grad_w_value: float32 [2048, 2048], P(None, 'tensor')
- grad_g_query: float32 [2048], P('tensor')
- grad_g_key: float32 [2048], P('tensor')
- grad_w_out: float32 [2048, 2048], P('tensor')
- grad_g_moe: float32 [2048], replicated
- grad_w_router: float32 [2048, 16], replicated
- grad_w_gate: float32 [16, 2048, 1024], P('expert', None, 'tensor')
- grad_w_up: float32 [16, 2048, 1024], P('expert', None, 'tensor')
- grad_w_down: float32 [16, 1024, 2048], P('expert', 'tensor')
Inputs may be any that keep to these rules, and one draw needn't show every extreme that they name: `lengths`: some slot has length 1024 and some has length 256. `routes`: the 8 experts of a token differ; among the rows of one device (aligned blocks of 1024 rows) no expert is named more than 576 times, a bound that some block reaches.
All inputs are finite; a program needn't handle non-finite values.
Results may differ from a plain program's by a relative error of at most 0.028.
Values may be sent and summed in bfloat16 or wider, within the bound.
No kernel may reach another device: no remote copies, remote signals or barrier semaphores. Data moves between devices by JAX's collectives and lax.ppermute only.
A program may use at most 576 MiB of HBM per device.

v0:
```python
import jax
import jax.numpy as jnp
from jax import lax
from jax.sharding import PartitionSpec as P

HD = 128
TOPK = 8
SLOT = 1024


EPS = 1e-05
THETA = 10000.0
NEGATIVE = -1e30


def cross_dot(operand, other_side):
    return lax.dot_general(
        operand, other_side, (((0,), (0,)), ((), ())), preferred_element_type=jnp.float32
    )


def dot_transposed(operand, other_side):
    return lax.dot_general(
        operand, other_side, (((1,), (1,)), ((), ())), preferred_element_type=jnp.float32
    )


def rotary_tables(length, head_size):
    frequency = THETA ** (-jnp.arange(0, head_size // 2, dtype=jnp.float32) * 2.0 / head_size)
    angles = jnp.arange(length, dtype=jnp.float32)[:, None] * frequency[None, :]
    return (jnp.cos(angles)[:, None, :], jnp.sin(angles)[:, None, :])


def rotate(values, cosine, sine_table):
    half_size = values.shape[-1] // 2
    first_half = values[..., :half_size]
    second = values[..., half_size:]
    return jnp.concatenate(
        [first_half * cosine - second * sine_table, second * cosine + first_half * sine_table],
        axis=-1,
    )


def unrotate(gradient, cosine, sine_table):
    half_size = gradient.shape[-1] // 2
    first_half = gradient[..., :half_size]
    second = gradient[..., half_size:]
    return jnp.concatenate(
        [first_half * cosine + second * sine_table, second * cosine - first_half * sine_table],
        axis=-1,
    )


def norm_back(grad_hat, values_hat, scale_rows):
    return scale_rows * (
        grad_hat - values_hat * jnp.mean(grad_hat * values_hat, axis=-1, keepdims=True)
    )


def block_scores(query_block, key_prefix, block_start, length, factor):
    raw_scores = jnp.einsum(
        "qhd,khd->hqk", query_block, key_prefix, preferred_element_type=jnp.float32
    )
    query_pos = block_start + jnp.arange(query_block.shape[0])
    key_pos = jnp.arange(key_prefix.shape[0])
    allowed = (key_pos[None, :] <= query_pos[:, None]) & (key_pos[None, :] < length)
    return (raw_scores * factor, allowed[None])


def padded_rows(array_rows):
    return jnp.concatenate(
        [array_rows, jnp.zeros((1, array_rows.shape[1]), array_rows.dtype)], axis=0
    )


def expert_forward(expert_rows, gate_weight, up_weight, down_weight):
    gate_pre = jnp.einsum(
        "secd,edf->secf", expert_rows, gate_weight, preferred_element_type=jnp.float32
    )
    up_pre = jnp.einsum(
        "secd,edf->secf", expert_rows, up_weight, preferred_element_type=jnp.float32
    )
    inner = (jax.nn.silu(gate_pre) * up_pre).astype(jnp.bfloat16)
    return jnp.einsum("secf,efd->secd", inner, down_weight, preferred_element_type=jnp.float32)


def expert_backward(expert_rows, d_expert, gate_weight, up_weight, down_weight):
    gate_back = jnp.einsum(
        "secd,edf->secf", expert_rows, gate_weight, preferred_element_type=jnp.float32
    )
    up_back = jnp.einsum(
        "secd,edf->secf", expert_rows, up_weight, preferred_element_type=jnp.float32
    )
    sigma = jax.nn.sigmoid(gate_back)
    silu_value = gate_back * sigma
    inner_back = (silu_value * up_back).astype(jnp.bfloat16)
    d_inner = jnp.einsum(
        "secd,efd->secf", d_expert, down_weight, preferred_element_type=jnp.float32
    )
    grad_down = jnp.einsum(
        "secf,secd->efd", inner_back, d_expert, preferred_element_type=jnp.float32
    )
    d_gate_pre = (d_inner * up_back * sigma * (1.0 + gate_back * (1.0 - sigma))).astype(
        jnp.bfloat16
    )
    d_up_pre = (d_inner * silu_value).astype(jnp.bfloat16)
    grad_gate = jnp.einsum(
        "secd,secf->edf", expert_rows, d_gate_pre, preferred_element_type=jnp.float32
    )
    grad_up = jnp.einsum(
        "secd,secf->edf", expert_rows, d_up_pre, preferred_element_type=jnp.float32
    )
    d_partial = jnp.einsum(
        "secf,edf->secd", d_gate_pre, gate_weight, preferred_element_type=jnp.float32
    ) + jnp.einsum("secf,edf->secd", d_up_pre, up_weight, preferred_element_type=jnp.float32)
    return (grad_gate, grad_up, grad_down, d_partial)


def shards(
    block_input,
    cotangent,
    lengths,
    routes,
    g_attn,
    w_query,
    w_key,
    w_value,
    g_query,
    g_key,
    w_out,
    g_moe,
    w_router,
    w_gate,
    w_up,
    w_down,
):
    tok_rows = block_input.shape[0]
    slice_width = block_input.shape[1]
    n_tensor = lax.axis_size("tensor")
    n_expert = lax.axis_size("expert")
    model_width = slice_width * n_tensor
    n_experts = w_router.shape[1]
    local_experts = w_gate.shape[0]
    capacity = n_tensor * (9 * tok_rows * TOPK // (8 * n_experts * n_tensor))
    heads_here = w_query.shape[1] // HD
    n_slots = lengths.shape[0]
    factor = HD ** (-0.5)
    tensor_index = lax.axis_index("tensor")
    offset = tensor_index * slice_width
    block_rows = min(512, SLOT)
    full_input, full_dy = (
        lax.all_gather(block_input, "tensor", axis=1, tiled=True),
        lax.all_gather(cotangent, "tensor", axis=1, tiled=True),
    )
    positions = jnp.arange(tok_rows) % SLOT
    live_rows = positions < jnp.repeat(lengths, SLOT, total_repeat_length=tok_rows)
    valid_rows = live_rows.astype(jnp.float32)[:, None]
    input_full = full_input.astype(jnp.float32)
    scale_x = lax.rsqrt(jnp.mean(input_full * input_full, axis=-1, keepdims=True) + EPS)
    x_hat = input_full * scale_x
    normed = (x_hat * g_attn).astype(jnp.bfloat16)
    q_raw = jnp.dot(normed, w_query, preferred_element_type=jnp.float32)
    k_raw = jnp.dot(normed, w_key, preferred_element_type=jnp.float32)
    values = jnp.dot(normed, w_value, preferred_element_type=jnp.float32).astype(jnp.bfloat16)
    q_total, k_total = lax.psum(
        (jnp.sum(q_raw * q_raw, axis=1), jnp.sum(k_raw * k_raw, axis=1)), "tensor"
    )
    scale_q = lax.rsqrt(q_total / model_width + EPS)[:, None]
    scale_k = lax.rsqrt(k_total / model_width + EPS)[:, None]
    q_norm = q_raw * scale_q * g_query
    k_norm = k_raw * scale_k * g_key
    cosine, sine_table = rotary_tables(SLOT, HD)
    head_shape = (n_slots, SLOT, heads_here, HD)
    query_heads = rotate(q_norm.reshape(head_shape), cosine, sine_table).astype(jnp.bfloat16)
    key_heads = rotate(k_norm.reshape(head_shape), cosine, sine_table).astype(jnp.bfloat16)
    value_heads = values.reshape(head_shape)
    outputs = []
    log_totals = []
    slot_index = 0
    for block_start in range(0, SLOT, block_rows):
        block_end = block_start + block_rows
        scores, allowed = block_scores(
            query_heads[slot_index, block_start:block_end],
            key_heads[slot_index, :block_end],
            block_start,
            lengths[slot_index],
            factor,
        )
        masked = jnp.where(allowed, scores, NEGATIVE)
        row_max = jnp.max(masked, axis=-1, keepdims=True)
        exponent_terms = jnp.exp(masked - row_max)
        row_total = jnp.sum(exponent_terms, axis=-1, keepdims=True)
        weights = (exponent_terms / row_total).astype(jnp.bfloat16)
        outputs.append(
            jnp.einsum(
                "hqk,khd->qhd",
                weights,
                value_heads[slot_index, :block_end],
                preferred_element_type=jnp.float32,
            )
        )
        log_totals.append(row_max + jnp.log(row_total))
    heads_out = (
        jnp.concatenate(outputs, axis=0).reshape(tok_rows, heads_here * HD).astype(jnp.bfloat16)
    )
    attn_part = jnp.dot(heads_out, w_out, preferred_element_type=jnp.float32)
    attn_full = lax.psum(attn_part, "tensor")
    hidden = input_full + attn_full
    scale_h = lax.rsqrt(jnp.mean(hidden * hidden, axis=-1, keepdims=True) + EPS)
    h_hat = hidden * scale_h
    moe_in = (h_hat * g_moe).astype(jnp.bfloat16)
    logits = jnp.dot(moe_in, w_router, preferred_element_type=jnp.float32)
    router_probs = jax.nn.softmax(logits, axis=-1)
    chosen = (routes[:, :, None] == jnp.arange(n_experts, dtype=jnp.int32)[None, None, :]).astype(
        jnp.float32
    )
    gates = (
        jnp.einsum("te,tje->tj", router_probs, chosen, precision=lax.Precision.HIGHEST) * valid_rows
    )
    pair_count = tok_rows * TOPK
    flat_routes = routes.reshape(pair_count)
    pair_live = jnp.repeat(live_rows, TOPK, total_repeat_length=pair_count)
    hits = (
        (flat_routes[:, None] == jnp.arange(n_experts, dtype=jnp.int32)[None, :])
        & pair_live[:, None]
    ).astype(jnp.int32)
    before = jnp.cumsum(hits, axis=0) - hits
    place = jnp.sum(before * hits, axis=1)
    slot_count = n_experts * capacity
    target = jnp.where(pair_live, flat_routes * capacity + place, slot_count)
    pair_of_slot = (
        jnp.full((slot_count,), pair_count, jnp.int32)
        .at[target]
        .set(jnp.arange(pair_count, dtype=jnp.int32), mode="drop")
    )
    token_of_slot = pair_of_slot // TOPK
    in_padded = padded_rows(moe_in)
    flat_gates = jnp.concatenate([gates.reshape(pair_count), jnp.zeros((1,), jnp.float32)])
    dy_padded = padded_rows(full_dy)
    d_out = full_dy.astype(jnp.float32) * valid_rows
    rows_per_owner = local_experts * capacity
    gate_of_slot = flat_gates[pair_of_slot]
    send_rows = in_padded[token_of_slot].reshape(n_expert, rows_per_owner, model_width)
    d_send = (
        (gate_of_slot[:, None] * dy_padded[token_of_slot].astype(jnp.float32))
        .astype(jnp.bfloat16)
        .reshape(n_expert, rows_per_owner, model_width)
    )
    received = lax.all_to_all(send_rows, "expert", split_axis=0, concat_axis=0, tiled=True)
    kept_rows = received.reshape(n_expert, local_experts, capacity, model_width)
    partial_out = expert_forward(kept_rows, w_gate, w_up, w_down)
    out_slice = lax.psum_scatter(
        partial_out.astype(jnp.bfloat16), "tensor", scatter_dimension=3, tiled=True
    )
    back_send = out_slice.reshape(n_expert, rows_per_owner, slice_width)
    returned = lax.all_to_all(back_send, "expert", split_axis=0, concat_axis=0, tiled=True)
    pair_out = (
        padded_rows(returned.reshape(slot_count, slice_width))[target]
        .reshape(tok_rows, TOPK, slice_width)
        .astype(jnp.float32)
    )
    moe_slice = jnp.sum(gates[:, :, None] * pair_out, axis=1)
    d_out_slice = lax.dynamic_slice_in_dim(d_out, offset, slice_width, 1)
    d_gate_part = jnp.sum(d_out_slice[:, None, :] * pair_out, axis=2)
    hidden_slice = lax.dynamic_slice_in_dim(hidden, offset, slice_width, 1)
    output = (valid_rows * (hidden_slice + moe_slice)).astype(jnp.bfloat16)
    d_gates = lax.psum(d_gate_part.astype(jnp.bfloat16), "tensor").astype(jnp.float32)
    rows_back, d_received = (
        lax.all_to_all(send_rows, "expert", split_axis=0, concat_axis=0, tiled=True),
        lax.all_to_all(d_send, "expert", split_axis=0, concat_axis=0, tiled=True),
    )
    expert_rows = rows_back.reshape(n_expert, local_experts, capacity, model_width)
    d_expert = d_received.reshape(n_expert, local_experts, capacity, model_width)
    grad_w_gate, grad_w_up, grad_w_down, d_partial = expert_backward(
        expert_rows, d_expert, w_gate, w_up, w_down
    )
    d_slice = lax.psum_scatter(
        d_partial.astype(jnp.bfloat16), "tensor", scatter_dimension=3, tiled=True
    )
    grad_send = d_slice.reshape(n_expert, rows_per_owner, slice_width)
    d_back = lax.all_to_all(grad_send, "expert", split_axis=0, concat_axis=0, tiled=True)
    d_pairs = padded_rows(d_back.reshape(slot_count, slice_width))[target].reshape(
        tok_rows, TOPK, slice_width
    )
    d_rows_slice = jnp.sum(d_pairs.astype(jnp.float32), axis=1)
    d_rows = lax.all_gather(d_rows_slice.astype(jnp.bfloat16), "tensor", axis=1, tiled=True).astype(
        d_rows_slice.dtype
    )
    d_probs = jnp.einsum(
        "tj,tje->te", d_gates * valid_rows, chosen, precision=lax.Precision.HIGHEST
    )
    d_logits = (
        router_probs * (d_probs - jnp.sum(router_probs * d_probs, axis=-1, keepdims=True))
    ).astype(jnp.bfloat16)
    grad_w_router = cross_dot(moe_in, d_logits)
    d_moe_in = dot_transposed(d_logits, w_router) + d_rows
    grad_g_moe = jnp.sum(d_moe_in * h_hat, axis=0)
    d_hidden = d_out + norm_back(d_moe_in * g_moe, h_hat, scale_h)
    d_attn = d_hidden.astype(jnp.bfloat16)
    grad_w_out = cross_dot(heads_out, d_attn)
    d_heads = dot_transposed(d_attn, w_out).astype(jnp.bfloat16).reshape(head_shape)
    d_query_parts = []
    block_number = 0
    slot_index = 0
    d_key_sum = jnp.zeros((SLOT, heads_here, HD), jnp.float32)
    d_value_sum = jnp.zeros((SLOT, heads_here, HD), jnp.float32)
    for block_start in range(0, SLOT, block_rows):
        block_end = block_start + block_rows
        query_block = query_heads[slot_index, block_start:block_end]
        key_prefix = key_heads[slot_index, :block_end]
        value_prefix = value_heads[slot_index, :block_end]
        scores, allowed = block_scores(
            query_block, key_prefix, block_start, lengths[slot_index], factor
        )
        probs = jnp.where(allowed, jnp.exp(scores - log_totals[block_number]), 0.0)
        block_number += 1
        d_block = d_heads[slot_index, block_start:block_end]
        d_probs_att = jnp.einsum(
            "qhd,khd->hqk", d_block, value_prefix, preferred_element_type=jnp.float32
        )
        spread = jnp.sum(probs * d_probs_att, axis=-1, keepdims=True)
        d_scores = (factor * probs * (d_probs_att - spread)).astype(jnp.bfloat16)
        d_query_parts.append(
            jnp.einsum("hqk,khd->qhd", d_scores, key_prefix, preferred_element_type=jnp.float32)
        )
        d_key_sum = d_key_sum.at[:block_end].add(
            jnp.einsum("hqk,qhd->khd", d_scores, query_block, preferred_element_type=jnp.float32)
        )
        d_value_sum = d_value_sum.at[:block_end].add(
            jnp.einsum(
                "hqk,qhd->khd",
                probs.astype(jnp.bfloat16),
                d_block,
                preferred_element_type=jnp.float32,
            )
        )
    d_key_slots = [d_key_sum]
    d_value_slots = [d_value_sum]
    d_query = jnp.concatenate(d_query_parts, axis=0).reshape(head_shape)
    d_keys = jnp.stack(d_key_slots, axis=0)
    d_values = (
        jnp.stack(d_value_slots, axis=0).reshape(tok_rows, heads_here * HD).astype(jnp.bfloat16)
    )
    d_q_norm = unrotate(d_query, cosine, sine_table).reshape(tok_rows, heads_here * HD)
    d_k_norm = unrotate(d_keys, cosine, sine_table).reshape(tok_rows, heads_here * HD)
    q_sum, k_sum = lax.psum(
        (jnp.sum(d_q_norm * g_query * q_raw, axis=1), jnp.sum(d_k_norm * g_key * k_raw, axis=1)),
        "tensor",
    )
    grad_g_query = jnp.sum(d_q_norm * q_raw * scale_q, axis=0)
    grad_g_key = jnp.sum(d_k_norm * k_raw * scale_k, axis=0)
    d_q_raw = (
        scale_q * g_query * d_q_norm - q_raw * scale_q**3 * (q_sum / model_width)[:, None]
    ).astype(jnp.bfloat16)
    d_k_raw = (
        scale_k * g_key * d_k_norm - k_raw * scale_k**3 * (k_sum / model_width)[:, None]
    ).astype(jnp.bfloat16)
    grad_w_query = cross_dot(normed, d_q_raw)
    grad_w_key = cross_dot(normed, d_k_raw)
    grad_w_value = cross_dot(normed, d_values)
    d_normed_part = (
        dot_transposed(d_q_raw, w_query)
        + dot_transposed(d_k_raw, w_key)
        + dot_transposed(d_values, w_value)
    )
    d_normed = lax.psum(d_normed_part.astype(jnp.bfloat16), "tensor").astype(jnp.float32)
    grad_g_attn = jnp.sum(d_normed * x_hat, axis=0)
    d_input = d_hidden + norm_back(d_normed * g_attn, x_hat, scale_x)
    grad_input = lax.dynamic_slice_in_dim(d_input, offset, slice_width, 1).astype(jnp.bfloat16)
    (
        sum_query,
        sum_key,
        sum_value,
        sum_out,
        sum_g_attn,
        sum_g_query,
        sum_g_key,
        sum_g_moe,
        sum_router,
    ) = (
        lax.psum(grad_w_query.astype(jnp.bfloat16), "expert").astype(jnp.float32),
        lax.psum(grad_w_key.astype(jnp.bfloat16), "expert").astype(jnp.float32),
        lax.psum(grad_w_value.astype(jnp.bfloat16), "expert").astype(jnp.float32),
        lax.psum(grad_w_out.astype(jnp.bfloat16), "expert").astype(jnp.float32),
        lax.psum(grad_g_attn.astype(jnp.bfloat16), "expert").astype(jnp.float32),
        lax.psum(grad_g_query.astype(jnp.bfloat16), "expert").astype(jnp.float32),
        lax.psum(grad_g_key.astype(jnp.bfloat16), "expert").astype(jnp.float32),
        lax.psum(grad_g_moe.astype(jnp.bfloat16), "expert").astype(jnp.float32),
        lax.psum(grad_w_router.astype(jnp.bfloat16), "expert").astype(jnp.float32),
    )
    return (
        output,
        grad_input,
        sum_g_attn,
        sum_query,
        sum_key,
        sum_value,
        sum_g_query,
        sum_g_key,
        sum_out,
        sum_g_moe,
        sum_router,
        grad_w_gate,
        grad_w_up,
        grad_w_down,
    )


def solution(mesh):
    placed = (
        P("expert", "tensor"),
        P("expert", "tensor"),
        P("expert"),
        P("expert", None),
        P(),
        P(None, "tensor"),
        P(None, "tensor"),
        P(None, "tensor"),
        P("tensor"),
        P("tensor"),
        P("tensor", None),
        P(),
        P(),
        P("expert", None, "tensor"),
        P("expert", None, "tensor"),
        P("expert", "tensor", None),
    )
    return jax.shard_map(
        shards,
        mesh=mesh,
        in_specs=placed,
        out_specs=(
            P("expert", "tensor"),
            P("expert", "tensor"),
            P(),
            P(None, "tensor"),
            P(None, "tensor"),
            P(None, "tensor"),
            P("tensor"),
            P("tensor"),
            P("tensor", None),
            P(),
            P(),
            P("expert", None, "tensor"),
            P("expert", None, "tensor"),
            P("expert", "tensor", None),
        ),
        check_vma=False,
    )
```

profile of v0, /device:TPU:0, one launch (start us, length us, event | category | flops | bytes accessed | tf_op | source)
XLA Modules:
  0.0 3366.6 jit_solution(5913606202694602335)
XLA Ops:
  12.0 34.8 %all-gather.4.cloned.1.call-done = bf16[1024,2048]{1,0:T(8,128)(2,1)} async-done(((bf16[1024,512]{1,0:T(8,128)(2,1)}), bf16[1024,2048]{1,0:T(8,128)(2,1)}) %all-gather.4.cloned.1.call-update) | async-done | bytes 4194320 | tf_op jit(solution)/shard_map/all_gather | solution.py:152
  50.2 5.7 multiply_reduce_fusion.7
  59.8 6.2 all-reduce.7
  111.2 5.7 fusion.141
  118.9 50.7 %gather_fusion = pred[8192]{0:T(1024)(128)(4,1)S(1)} fusion(pred[1024]{0:T(1024)(128)(4,1)S(1)} %fusion.118, s32[8192]{0:T(1024)S(1)} %broadcast_clamp_fusion.1), kind=kCustom, calls=%fused_computation | custom fusion | bytes 49152 | tf_op jit(solution)/shard_map/jit(_take)/gather | solution.py:222
  176.5 30.9 scatter_custom_fusion
  208.1 62.9 %all-reduce.14.cloned.1.call-done = f32[1024,2048]{1,0:T(8,128)} async-done(((f32[1024,2048]{1,0:T(8,128)}), f32[1024,2048]{1,0:T(8,128)}) %all-reduce.14.cloned.1.call-update) | async-done | bytes 8388624 | tf_op jit(solution)/shard_map/psum | solution.py:207
  271.0 5.7 multiply_reduce_fusion.4
  283.3 71.6 %gather_fusion.1 = bf16[9216,2048]{1,0:T(8,128)(2,1)} fusion(bf16[1025,2048]{1,0:T(8,128)(2,1)} %concatenate.82, s32[9216]{0:T(1024)S(1)} %get-tuple-element.163), kind=kCustom, calls=%fused_computation.1 | custom fusion | bytes 75534336 | tf_op jit(solution)/shard_map/gather | solution.py:243
  354.8 7.6 all-to-all-start
  363.2 36.5 %all-gather.6.cloned.1.call-done = bf16[1024,2048]{1,0:T(8,128)(2,1)} async-done(((bf16[1024,512]{1,0:T(8,128)(2,1)}), bf16[1024,2048]{1,0:T(8,128)(2,1)}) %all-gather.6.cloned.1.call-update) | async-done | bytes 4194320 | tf_op jit(solution)/shard_map/all_gather | solution.py:153
  404.5 71.6 %gather_fusion.4 = bf16[9216,2048]{1,0:T(8,128)(2,1)} fusion(bf16[1025,2048]{1,0:T(8,128)(2,1)} %concatenate.85, s32[9216]{0:T(1024)S(1)} %get-tuple-element.163), kind=kCustom, calls=%fused_computation.4 | custom fusion | bytes 75534336 | tf_op jit(solution)/shard_map/gather | solution.py:245
  481.8 51.2 %gather_fusion.3 = f32[9216]{0:T(1024)S(1)} fusion(f32[8193]{0:T(1024)S(1)} %pad_maximum_fusion.8, s32[9216]{0:T(1024)S(1)} %copy-done.63), kind=kCustom, calls=%fused_computation.3 | custom fusion | bytes 110592 | tf_op jit(solution)/shard_map/gather | solution.py:242
  532.9 25.5 fusion
  558.4 616.2 %all-to-all-done = bf16[8,1152,2048]{2,1,0:T(8,128)(2,1)} async-done(((bf16[8,1152,2048]{2,1,0:T(8,128)(2,1)}), bf16[8,1152,2048]{2,1,0:T(8,128)(2,1)}, u32[]{:S(2)}, u32[]{:S(2)}) %all-to-all-start) | async-done | bytes 37748768 | tf_op jit(solution)/shard_map/all_to_all | solution.py:249
  1174.7 7.4 all-to-all-start.2
  1182.3 20.8 fusion.6
  1203.1 20.2 fusion.8
  1223.3 770.2 %all-to-all-done.2 = bf16[8,1152,2048]{2,1,0:T(8,128)(2,1)} async-done(((bf16[8,1152,2048]{2,1,0:T(8,128)(2,1)}), bf16[8,1152,2048]{2,1,0:T(8,128)(2,1)}, u32[]{:S(2)}, u32[]{:S(2)}) %all-to-all-start.2) | async-done | bytes 37748768 | tf_op jit(solution)/shard_map/all_to_all | solution.py:270
  1993.5 25.9 fusion.15
  2019.4 29.8 fusion.67
  2049.1 40.2 %fusion.1 = bf16[8,2,576,2048]{3,2,0,1:T(8,128)(2,1)} fusion(f32[2,8,576,2048]{3,2,1,0:T(8,128)} %fusion.67, bf16[8,2,576,256]{3,2,0,1:T(8,128)(2,1)} %get-tuple-element.139, bf16[2,2048,256]{2,1,0:T(8,128)(2,1)} %param.48), kind=kOutput, calls=%fused_computation.10 | convolution fusion | flops 9701425152 | bytes 120061952 | tf_op jit(solution)/shard_map/secf,edf->secd/dot_general | solution.py:115
  2089.4 28.7 convert_bitcast_fusion
  2118.1 227.8 %reduce-scatter.5.cloned.1.call-done = bf16[8,2,576,512]{3,2,0,1:T(8,128)(2,1)} async-done(((bf16[8,2,576,2048]{3,2,0,1:T(8,128)(2,1)}), bf16[8,2,576,512]{3,2,0,1:T(8,128)(2,1)}) %reduce-scatter.5.cloned.1.call-update) | async-done | bytes 9437200 | tf_op jit(solution)/shard_map/reduce_scatter | solution.py:277
  2345.9 8.4 copy.103
  2359.7 246.2 %reduce-scatter.3.cloned.1.call-done = bf16[8,2,576,512]{3,2,0,1:T(8,128)(2,1)} async-done(((bf16[8,2,576,2048]{3,2,0,1:T(8,128)(2,1)}), bf16[8,2,576,512]{3,2,0,1:T(8,128)(2,1)}) %reduce-scatter.3.cloned.1.call-update) | async-done | bytes 9437200 | tf_op jit(solution)/shard_map/reduce_scatter | solution.py:252
  2605.8 8.2 copy.101
  2614.0 5.7 all-to-all-start.1
  2619.7 9.6 concatenate.86
  2629.3 38.8 %gather_fusion.5 = bf16[8192,512]{1,0:T(8,128)(2,1)} fusion(bf16[9217,512]{1,0:T(8,128)(2,1)} %concatenate.86, s32[8192]{0:T(1024)S(1)} %broadcast_clamp_fusion), kind=kCustom, calls=%fused_computation.5 | custom fusion | bytes 16809984 | tf_op jit(solution)/shard_map/gather | solution.py:282
  2668.1 10.0 bitcast_reduce_fusion
  2682.6 142.5 %all-to-all-done.1 = bf16[8,1152,512]{2,1,0:T(8,128)(2,1)} async-done(((bf16[8,1152,512]{2,1,0:T(8,128)(2,1)}), bf16[8,1152,512]{2,1,0:T(8,128)(2,1)}, u32[]{:S(2)}, u32[]{:S(2)}) %all-to-all-start.1) | async-done | bytes 9437216 | tf_op jit(solution)/shard_map/all_to_all | solution.py:256
  2825.1 9.4 concatenate.83
  2834.5 38.8 %gather_fusion.2 = bf16[8192,512]{1,0:T(8,128)(2,1)} fusion(bf16[9217,512]{1,0:T(8,128)(2,1)} %concatenate.83, s32[8192]{0:T(1024)S(1)} %broadcast_clamp_fusion), kind=kCustom, calls=%fused_computation.2 | custom fusion | bytes 16809984 | tf_op jit(solution)/shard_map/gather | solution.py:258
  2873.3 11.6 fusion.11
  2884.9 13.8 psum.115
  2902.8 6.9 multiply_reduce_fusion
  2909.7 5.8 multiply_add_fusion
  2915.5 5.7 fusion.83
  2960.8 6.0 all-reduce.6
  2976.2 6.4 add_convert_fusion.1
  2983.8 6.6 convolution_convert_fusion.1
  3002.5 22.5 fusion.42
  3024.9 22.2 fusion.39
  3047.1 19.4 fusion.36
  3069.4 9.4 fusion.21
  3078.8 37.9 %all-reduce.8 = (bf16[2048]{0:T(1024)(128)(2,1)S(1)}, bf16[512]{0:T(512)(128)(2,1)S(1)}, bf16[512]{0:T(512)(128)(2,1)S(1)}, bf16[2048]{0:T(1024)(128)(2,1)S(1)}) all-reduce(bf16[2048]{0:T(1024)(128)(2,1)S(1)} %get-tuple-element.116, bf16[512]{0:T(512)(128)(2,1)S(1)} %get-tuple-element.122, ...), channel_id=1, replica_groups=mesh['expert'=8,'tensor'=4] {'expert'}, use_global_device_ids=true, to_apply=%region_34.35 | all-reduce | flops 5120 | bytes 20480 | tf_op jit(solution)/shard_map/psum | solution.py:385
  3123.3 222.3 %all-reduce.18.cloned.1.call-done = (bf16[2048,512]{1,0:T(8,128)(2,1)}, bf16[2048,512]{1,0:T(8,128)(2,1)}, bf16[2048,512]{1,0:T(8,128)(2,1)}, bf16[512,2048]{1,0:T(8,128)(2,1)}, bf16[2048,16]{0,1:T(8,128)(2,1)}) async-done(((bf16[2048,512]{1,0:T(8,128)(2,1)}, bf16[2048,512]{1,0:T(8,128)(2,1)}, bf16[2048,512]{1,0:T(8,128)(2,1)}, bf16[512,2048]{1,0:T(8,128)(2,1)}, bf16[2048,16]{0,1:T(8,128)(2,1)}), ...) | async-done | bytes 8454160 | tf_op jit(solution)/shard_map/psum | solution.py:381
  (344 shorter events, 182.5 us)
Async XLA Ops:
  7.2 1986.3 %copy-start = (bf16[2,256,2048]{2,1,0:T(8,128)(2,1)S(1)}, bf16[2,256,2048]{2,1,0:T(8,128)(2,1)}, u32[]{:S(2)}) copy-start(bf16[2,256,2048]{2,1,0:T(8,128)(2,1)} %param.49) | copy-start | bytes 6291460
  7.2 42.8 %copy-start.95 = (f32[2048]{0:T(1024)S(1)}, f32[2048]{0:T(1024)}, u32[]{:S(2)}) copy-start(f32[2048]{0:T(1024)} %param.38) | copy-start | bytes 24580
  7.2 39.6 %all-gather.4.cloned.1.call-start = ((), (), s32[]{:S(2)}) async-start(), calls=%async_computation.6 | async-start | bytes 5242880 | tf_op jit(solution)/shard_map/all_gather | solution.py:152
  7.9 263.1 %all-reduce.14.cloned.1.call-start = ((), (), s32[]{:S(2)}) async-start(), calls=%async_computation.7 | async-start | bytes 16777216 | tf_op jit(solution)/shard_map/psum | solution.py:207
  8.8 90.5 %copy-start.26 = (pred[512,512]{0,1:T(8,128)(4,1)}, pred[512,512]{0,1:T(8,128)(4,1)S(1)}, u32[]{:S(2)}) copy-start(pred[512,512]{0,1:T(8,128)(4,1)S(1)} %fusion.93) | copy-start | bytes 786436
  9.2 96.6 %copy-start.17 = (pred[512,1024]{1,0:T(8,128)(4,1)}, pred[512,1024]{1,0:T(8,128)(4,1)S(1)}, u32[]{:S(2)}) copy-start(pred[512,1024]{1,0:T(8,128)(4,1)S(1)} %fusion.78) | copy-start | bytes 1572868
  12.0 73.9 %copy-start.34 = (f32[1024,64]{1,0:T(8,128)}, f32[1024,64]{1,0:T(8,128)S(1)}, u32[]{:S(2)}) copy-start(f32[1024,64]{1,0:T(8,128)S(1)} %get-tuple-element.168) | copy-start | bytes 786436
  50.2 43.3 %copy-start.81 = (f32[1024]{0:T(1024)}, f32[1024]{0:T(1024)S(1)}, u32[]{:S(2)}) copy-start(f32[1024]{0:T(1024)S(1)} %add_rsqrt_fusion.3) | copy-start | bytes 12292
  55.9 10.8 copy-start.90
  66.7 9.6 copy-start.79
  70.0 6.3 copy-start.88
  90.7 10.2 copy-start.19
  90.7 10.2 copy-start.21
  91.3 9.6 copy-start.32
  92.5 6.8 copy-start.4
  92.5 6.8 copy-start.69
  99.3 6.5 copy-start.37
  208.1 68.6 %copy-start.67 = (f32[2048]{0:T(1024)S(1)}, f32[2048]{0:T(1024)}, u32[]{:S(2)}) copy-start(f32[2048]{0:T(1024)} %param.45) | copy-start | bytes 24580
  354.8 819.8 %all-to-all-start = ((bf16[8,1152,2048]{2,1,0:T(8,128)(2,1)}), bf16[8,1152,2048]{2,1,0:T(8,128)(2,1)}, u32[]{:S(2)}, u32[]{:S(2)}) async-start(bf16[8,1152,2048]{2,1,0:T(8,128)(2,1)} %bitcast.254), calls=%async_computation | async-start | bytes 75497472 | tf_op jit(solution)/shard_map/all_to_all | solution.py:249
  362.5 37.2 %all-gather.6.cloned.1.call-start = ((), (), s32[]{:S(2)}) async-start(), calls=%async_computation.9 | async-start | bytes 5242880 | tf_op jit(solution)/shard_map/all_gather | solution.py:153
  363.2 117.3 %copy-start.60 = (f32[1024]{0:T(1024)}, f32[1024]{0:T(1024)S(1)}, u32[]{:S(2)}) copy-start(f32[1024]{0:T(1024)S(1)} %fusion.122) | copy-start | bytes 12292
  404.5 71.6 %copy-start.58 = (bf16[2048,16]{0,1:T(8,128)(2,1)S(1)}, bf16[2048,16]{0,1:T(8,128)(2,1)}, u32[]{:S(2)}) copy-start(bf16[2048,16]{0,1:T(8,128)(2,1)} %param.46) | copy-start | bytes 196612
  1174.7 818.8 %all-to-all-start.2 = ((bf16[8,1152,2048]{2,1,0:T(8,128)(2,1)}), bf16[8,1152,2048]{2,1,0:T(8,128)(2,1)}, u32[]{:S(2)}, u32[]{:S(2)}) async-start(bf16[8,1152,2048]{2,1,0:T(8,128)(2,1)} %fusion), calls=%async_computation.3 | async-start | bytes 75497472 | tf_op jit(solution)/shard_map/all_to_all | solution.py:270
  1182.1 1163.8 %reduce-scatter.5.cloned.1.call-start = ((), (), s32[]{:S(2)}) async-start(), calls=%async_computation.10 | async-start | bytes 47185920 | tf_op jit(solution)/shard_map/reduce_scatter | solution.py:277
  1182.3 20.8 copy-start.39
  2089.3 516.5 %reduce-scatter.3.cloned.1.call-start = ((), (), s32[]{:S(2)}) async-start(), calls=%async_computation.8 | async-start | bytes 47185920 | tf_op jit(solution)/shard_map/reduce_scatter | solution.py:252
  2354.3 259.7 %all-to-all-start.3 = ((bf16[8,1152,512]{2,1,0:T(8,128)(2,1)}), bf16[8,1152,512]{2,1,0:T(8,128)(2,1)}, u32[]{:S(2)}, u32[]{:S(2)}) async-start(bf16[8,1152,512]{2,1,0:T(8,128)(2,1)} %bitcast.259), calls=%async_computation.5 | async-start | bytes 18874368 | tf_op jit(solution)/shard_map/all_to_all | solution.py:281
  2614.0 211.1 %all-to-all-start.1 = ((bf16[8,1152,512]{2,1,0:T(8,128)(2,1)}), bf16[8,1152,512]{2,1,0:T(8,128)(2,1)}, u32[]{:S(2)}, u32[]{:S(2)}) async-start(bf16[8,1152,512]{2,1,0:T(8,128)(2,1)} %bitcast.258), calls=%async_computation.2 | async-start | bytes 18874368 | tf_op jit(solution)/shard_map/all_to_all | solution.py:256
  2619.7 283.1 %all-gather.8.cloned.1.call-start = ((), (), s32[]{:S(2)}) async-start(), calls=%async_computation.11 | async-start | bytes 5242880 | tf_op jit(solution)/shard_map/all_gather | solution.py:286
  2668.1 10.1 copy-start.61
  2678.1 391.3 %all-reduce.16.cloned.1.call-start = ((), (), s32[]{:S(2)}) async-start(), calls=%async_computation.12 | async-start | bytes 8388608 | tf_op jit(solution)/shard_map/psum | solution.py:366
  2834.5 38.8 %copy-start.29 = (f32[1024,8]{1,0:T(8,128)S(1)}, f32[1024,8]{1,0:T(8,128)}, u32[]{:S(2)}) copy-start(f32[1024,8]{1,0:T(8,128)} %copy-done.28) | copy-start | bytes 98308
  2873.3 25.8 copy-start.57
  2873.3 25.9 copy-start.45
  2873.3 25.9 copy-start.66
  2873.3 25.9 copy-start.76
  2884.9 17.9 copy-start.59
  2884.9 17.9 copy-start.68
  2884.9 17.9 copy-start.74
  2902.8 6.9 copy-start.6
  2955.1 11.8 copy-start.94
  2982.6 363.0 %all-reduce.18.cloned.1.call-start = ((), (), s32[]{:S(2)}) async-start(), calls=%async_computation.13 | async-start | bytes 16908288 | tf_op jit(solution)/shard_map/psum | solution.py:381
  2983.8 6.6 copy-start.9
  2983.8 6.6 copy-start.54
  2990.4 8.4 slice-start.2
  3047.1 19.4 copy-start.25
  3047.1 19.4 copy-start.62
  3069.4 9.4 copy-start.92
  (69 other events, 205.5 us)
Sparse Core Ops, SparseCore 0:
  9.6 37.1 all-gather.3
  117.0 153.9 all-reduce.13
  364.8 34.8 all-gather.5
  2089.4 256.3 reduce-scatter.4
  2348.3 257.4 reduce-scatter.2
  2678.2 34.8 all-gather.7
  2982.7 84.8 all-reduce.15
  3073.7 271.8 all-reduce.17
where the time goes:
time: 3370 us
  waiting for transfers between devices  2360 us (70%)
  local copies, waits for them, and re-layouts  436 us (13%)
  matrix products  319 us (9%)
  other arithmetic  143 us (4%)
  blocking collectives  63.9 us (2%)
    all_to_all x1, waiting for transfers between devices, shards(): lax.all_to_all(d_send, 'expert', split_axis=0, concat_axis=0, tiled=True)  770 us
    all_to_all x1, waiting for transfers between devices, shards(): lax.all_to_all(send_rows, 'expert', split_axis=0, concat_axis=0, tiled=True)  616 us
    reduce_scatter x1, waiting for transfers between devices, shards(): lax.psum_scatter(partial_out.astype(jnp.bfloat16), 'tensor', scatter_dime...  246 us
    reduce_scatter x1, waiting for transfers between devices, shards(): lax.psum_scatter(d_partial.astype(jnp.bfloat16), 'tensor', scatter_dimens...  228 us
    psum x1, waiting for transfers between devices, shards(): lax.psum(grad_w_query.astype(jnp.bfloat16), 'expert').astype(jnp.float32)  222 us
    all_to_all x1, waiting for transfers between devices, shards(): lax.all_to_all(back_send, 'expert', split_axis=0, concat_axis=0, tiled=True)  143 us
    gather x1, local copies, waits for them, and re-layouts, shards(): dy_padded[token_of_slot].astype(jnp.float32)  71.6 us
    gather x1, local copies, waits for them, and re-layouts, shards(): in_padded[token_of_slot].reshape(n_expert, rows_per_owner, model_width)  71.6 us
  transfers between devices with their start and end apart: 12, of which 9 were waited for; matrix products, arithmetic and copies ran while one was open for 17% of the time, Pallas kernels for 0%

commit v1 on v0

v1 whole, which is shorter than its diff:
```python
import functools

import jax
import jax.numpy as jnp
from jax import lax
from jax.experimental import pallas as pl
from jax.experimental.pallas import tpu as pltpu
from jax.sharding import PartitionSpec as P

HD = 128
TOPK = 8
SLOT = 1024


EPS = 1e-05
THETA = 10000.0
NEGATIVE = -1e30


def cross_dot(operand, other_side):
    return lax.dot_general(
        operand, other_side, (((0,), (0,)), ((), ())), preferred_element_type=jnp.float32
    )


def dot_transposed(operand, other_side):
    return lax.dot_general(
        operand, other_side, (((1,), (1,)), ((), ())), preferred_element_type=jnp.float32
    )


def rotary_tables(length, head_size):
    frequency = THETA ** (-jnp.arange(0, head_size // 2, dtype=jnp.float32) * 2.0 / head_size)
    angles = jnp.arange(length, dtype=jnp.float32)[:, None] * frequency[None, :]
    return (jnp.cos(angles)[:, None, :], jnp.sin(angles)[:, None, :])


def rotate(values, cosine, sine_table):
    half_size = values.shape[-1] // 2
    first_half = values[..., :half_size]
    second = values[..., half_size:]
    return jnp.concatenate(
        [first_half * cosine - second * sine_table, second * cosine + first_half * sine_table],
        axis=-1,
    )


def unrotate(gradient, cosine, sine_table):
    half_size = gradient.shape[-1] // 2
    first_half = gradient[..., :half_size]
    second = gradient[..., half_size:]
    return jnp.concatenate(
        [first_half * cosine + second * sine_table, second * cosine - first_half * sine_table],
        axis=-1,
    )


def block_scores(query_block, key_prefix, block_start, length, factor):
    raw_scores = jnp.einsum(
        "qhd,khd->hqk", query_block, key_prefix, preferred_element_type=jnp.float32
    )
    query_pos = block_start + jnp.arange(query_block.shape[0])
    key_pos = jnp.arange(key_prefix.shape[0])
    allowed = (key_pos[None, :] <= query_pos[:, None]) & (key_pos[None, :] < length)
    return (raw_scores * factor, allowed[None])


def moe_body(
    resume,
    starts,
    lens,
    x_ref,
    g_ref,
    info_ref,
    wgu_ref,
    wd_ref,
    gate_before,
    up_before,
    down_before,
    out_ref,
    dx_ref,
    dgate_ref,
    gate_grad,
    up_grad,
    down_grad,
    acc_in,
    acc_down,
    sem,
):
    n_local, width = gate_grad.shape[0], gate_grad.shape[2]
    hidden = n_local * width
    pieces, rows, cols = x_ref.shape
    slot, block = pl.program_id(0), pl.program_id(1)

    def move(gate_hbm, up_hbm, down_hbm, store):
        pairs = []
        for e in range(n_local):
            at = pl.ds(e * width, width)
            pairs.append((acc_in.at[:, at], gate_hbm.at[e]))
            pairs.append((acc_in.at[:, pl.ds(hidden + e * width, width)], up_hbm.at[e]))
            pairs.append((acc_down.at[at, :], down_hbm.at[e]))
        started = []
        for k, (inside, outside) in enumerate(pairs):
            ends = (inside, outside) if store else (outside, inside)
            copy = pltpu.make_async_copy(*ends, sem.at[k])
            copy.start()
            started.append(copy)
        for copy in started:
            copy.wait()

    @pl.when((slot == 0) & (block == 0))
    def _():
        if resume:
            move(gate_before, up_before, down_before, False)
        else:
            acc_in[...] = jnp.zeros_like(acc_in)
            acc_down[...] = jnp.zeros_like(acc_down)

    live = starts[0] + block * rows < lens[slot]

    @pl.when(live)
    def _():
        scale = info_ref[:, n_local : n_local + 1]
        pre = jnp.zeros((rows, 2 * hidden), jnp.float32)
        d_raw = jnp.zeros((rows, hidden), jnp.float32)
        for p in range(pieces):
            span = slice(p * cols, (p + 1) * cols)
            pre += jnp.dot(x_ref[p], wgu_ref[span, :], preferred_element_type=jnp.float32)
            d_raw += dot_transposed(g_ref[p], wd_ref[:, span])
        inner_parts, gate_parts, up_parts = [], [], []
        for e in range(n_local):
            at = slice(e * width, (e + 1) * width)
            gate_pre = pre[:, at] * scale
            up_pre = pre[:, hidden + e * width : hidden + (e + 1) * width] * scale
            gate = info_ref[:, e : e + 1]
            sigma = jax.nn.sigmoid(gate_pre)
            silu_value = gate_pre * sigma
            inner = silu_value * up_pre
            raw = d_raw[:, at]
            dgate_ref[:, e : e + 1] = jnp.sum(inner * raw, axis=1, keepdims=True)
            d_inner = raw * (gate * scale)
            inner_parts.append((inner * gate).astype(jnp.bfloat16))
            gate_parts.append(
                (d_inner * up_pre * sigma * (1.0 + gate_pre * (1.0 - sigma))).astype(jnp.bfloat16)
            )
            up_parts.append((d_inner * silu_value).astype(jnp.bfloat16))
        inner_all = jnp.concatenate(inner_parts, axis=1)
        d_pre = jnp.concatenate(gate_parts + up_parts, axis=1)
        for p in range(pieces):
            span = slice(p * cols, (p + 1) * cols)
            out_ref[p] = jnp.dot(
                inner_all, wd_ref[:, span], preferred_element_type=jnp.float32
            ).astype(jnp.bfloat16)
            dx_ref[p] = dot_transposed(d_pre, wgu_ref[span, :]).astype(jnp.bfloat16)
            acc_in[span, :] += cross_dot(x_ref[p], d_pre)
            acc_down[:, span] += cross_dot(inner_all, g_ref[p])

    @pl.when(jnp.logical_not(live))
    def _():
        out_ref[...] = jnp.zeros_like(out_ref)
        dx_ref[...] = jnp.zeros_like(dx_ref)
        dgate_ref[...] = jnp.zeros_like(dgate_ref)

    @pl.when((slot == pl.num_programs(0) - 1) & (block == pl.num_programs(1) - 1))
    def _():
        move(gate_grad, up_grad, down_grad, True)


def moe_call(start, lens, x_all, g_all, info, wgu, wd, n_local, before):
    slots, pieces, rows, cols = x_all.shape
    width = wd.shape[0] // n_local
    model = pieces * cols
    tile = min(256, rows)

    def row_block(minor):
        return pl.BlockSpec((None, tile, minor), lambda s, b, *_: (s, b, 0))

    def piece_block():
        return pl.BlockSpec((None, pieces, tile, cols), lambda s, b, *_: (s, 0, b, 0))

    def whole(shape):
        return pl.BlockSpec(shape, lambda s, b, *_: (0, 0), pipeline_mode=pl.Buffered(1))

    f32 = jnp.float32
    anywhere = pl.BlockSpec(memory_space=pl.ANY)
    resume = before is not None
    if not resume:
        before = [jnp.zeros((8, 128), f32)] * 3
    return pl.pallas_call(
        functools.partial(moe_body, resume),
        out_shape=(
            jax.ShapeDtypeStruct(x_all.shape, jnp.bfloat16),
            jax.ShapeDtypeStruct(x_all.shape, jnp.bfloat16),
            jax.ShapeDtypeStruct(info.shape, f32),
            jax.ShapeDtypeStruct((n_local, model, width), f32),
            jax.ShapeDtypeStruct((n_local, model, width), f32),
            jax.ShapeDtypeStruct((n_local, width, model), f32),
        ),
        grid_spec=pltpu.PrefetchScalarGridSpec(
            num_scalar_prefetch=2,
            grid=(slots, rows // tile),
            in_specs=[
                piece_block(),
                piece_block(),
                row_block(info.shape[2]),
                whole(wgu.shape),
                whole(wd.shape),
                anywhere,
                anywhere,
                anywhere,
            ],
            out_specs=[
                piece_block(),
                piece_block(),
                row_block(info.shape[2]),
                anywhere,
                anywhere,
                anywhere,
            ],
            scratch_shapes=[
                pltpu.VMEM((model, wgu.shape[1]), f32),
                pltpu.VMEM(wd.shape, f32),
                pltpu.SemaphoreType.DMA((3 * n_local,)),
            ],
        ),
        input_output_aliases={7: 3, 8: 4, 9: 5} if resume else {},
        name="experts",
    )(start, lens, x_all, g_all, info, wgu, wd, *before)


def shards(
    block_input,
    cotangent,
    lengths,
    routes,
    g_attn,
    w_query,
    w_key,
    w_value,
    g_query,
    g_key,
    w_out,
    g_moe,
    w_router,
    w_gate,
    w_up,
    w_down,
):
    tok_rows, slice_width = block_input.shape
    n_tensor = lax.axis_size("tensor")
    n_expert = lax.axis_size("expert")
    everyone = ("expert", "tensor")
    model_width = slice_width * n_tensor
    n_experts = w_router.shape[1]
    n_local = w_gate.shape[0]
    heads_here = w_query.shape[1] // HD
    factor = HD ** (-0.5)
    e_index = lax.axis_index("expert")
    offset = lax.axis_index("tensor") * slice_width
    block_rows = min(512, SLOT)
    n_chunks = max(1, n_expert // 4) if n_expert > 8 else 1
    chunk_rows = tok_rows // n_chunks

    def own_columns(vector):
        return lax.dynamic_slice_in_dim(vector, offset, slice_width, vector.ndim - 1)

    full_input = lax.all_gather(block_input, "tensor", axis=1, tiled=True)
    early, _ = lax.optimization_barrier((cotangent, full_input))
    all_lengths = lax.all_gather(lengths, "expert", axis=0, tiled=True)
    positions = jnp.arange(tok_rows)
    live_rows = positions < lengths[0]
    valid_rows = live_rows.astype(jnp.float32)[:, None]
    input_full = full_input.astype(jnp.float32)
    scale_x = lax.rsqrt(jnp.mean(input_full * input_full, axis=-1, keepdims=True) + EPS)
    normed = (input_full * scale_x * g_attn).astype(jnp.bfloat16)
    q_raw = jnp.dot(normed, w_query, preferred_element_type=jnp.float32)
    k_raw = jnp.dot(normed, w_key, preferred_element_type=jnp.float32)
    values = jnp.dot(normed, w_value, preferred_element_type=jnp.float32).astype(jnp.bfloat16)
    q_total, k_total = lax.psum(
        (jnp.sum(q_raw * q_raw, axis=1), jnp.sum(k_raw * k_raw, axis=1)), "tensor"
    )
    scale_q = lax.rsqrt(q_total / model_width + EPS)[:, None]
    scale_k = lax.rsqrt(k_total / model_width + EPS)[:, None]
    q_norm = q_raw * scale_q * g_query
    k_norm = k_raw * scale_k * g_key
    cosine, sine_table = rotary_tables(SLOT, HD)
    head_shape = (SLOT, heads_here, HD)
    query_heads = rotate(q_norm.reshape(head_shape), cosine, sine_table).astype(jnp.bfloat16)
    key_heads = rotate(k_norm.reshape(head_shape), cosine, sine_table).astype(jnp.bfloat16)
    value_heads = values.reshape(head_shape)
    outputs = []
    log_totals = []
    for block_start in range(0, SLOT, block_rows):
        block_end = block_start + block_rows
        scores, allowed = block_scores(
            query_heads[block_start:block_end], key_heads[:block_end], block_start, lengths[0], factor
        )
        masked = jnp.where(allowed, scores, NEGATIVE)
        row_max = jnp.max(masked, axis=-1, keepdims=True)
        exponent_terms = jnp.exp(masked - row_max)
        row_total = jnp.sum(exponent_terms, axis=-1, keepdims=True)
        weights = (exponent_terms / row_total).astype(jnp.bfloat16)
        outputs.append(
            jnp.einsum(
                "hqk,khd->qhd", weights, value_heads[:block_end], preferred_element_type=jnp.float32
            )
        )
        log_totals.append(row_max + jnp.log(row_total))
    heads_out = (
        jnp.concatenate(outputs, axis=0).reshape(tok_rows, heads_here * HD).astype(jnp.bfloat16)
    )
    attn_part = jnp.dot(heads_out, w_out, preferred_element_type=jnp.float32).astype(jnp.bfloat16)
    attn_slice = lax.psum_scatter(attn_part, "tensor", scatter_dimension=1, tiled=True)
    hidden = block_input.astype(jnp.float32) + attn_slice.astype(jnp.float32)
    g_moe_slice = own_columns(g_moe)
    moe_rows = (hidden * g_moe_slice).astype(jnp.bfloat16)
    router_slice = lax.dynamic_slice_in_dim(w_router, offset, slice_width, 0)
    statistics = jnp.concatenate(
        [
            jnp.dot(moe_rows, router_slice, preferred_element_type=jnp.float32),
            jnp.sum(hidden * hidden, axis=1, keepdims=True),
        ],
        axis=1,
    )
    statistics = lax.psum(statistics, "tensor")
    scale_h = lax.rsqrt(statistics[:, n_experts:] / model_width + EPS)
    router_probs = jax.nn.softmax(statistics[:, :n_experts] * scale_h, axis=-1)
    expert_ids = jnp.arange(n_experts, dtype=jnp.int32)
    chosen = jnp.any(routes[:, :, None] == expert_ids[None, None, :], axis=1) & live_rows[:, None]
    chosen = chosen.astype(jnp.float32)
    gates = router_probs * chosen
    info = lax.all_gather(jnp.concatenate([gates, scale_h], axis=1).T, "expert", axis=0)
    info = jnp.concatenate(
        [
            lax.dynamic_slice_in_dim(info, e_index * n_local, n_local, 1),
            info[:, n_experts:],
            jnp.zeros((n_expert, 8 - n_local - 1, tok_rows), jnp.float32),
        ],
        axis=1,
    ).transpose(0, 2, 1)
    wgu = jnp.concatenate([w_gate[e] for e in range(n_local)] + [w_up[e] for e in range(n_local)], axis=1)
    wd = w_down.reshape(-1, model_width)

    moe_parts, back_parts, dgate_parts, own_rows, own_dy = [], [], [], [], []
    weight_grads = None
    chain = None
    for chunk in range(n_chunks):
        at = slice(chunk * chunk_rows, (chunk + 1) * chunk_rows)
        x_piece, g_piece = moe_rows[at], early[at]
        if chain is not None:
            x_piece, g_piece, chain = lax.optimization_barrier((x_piece, g_piece, chain))
            back_parts[-1], moe_parts[-1], own_rows[-1], own_dy[-1], weight_grads = chain
        shape = (n_expert, n_tensor, chunk_rows, slice_width)
        g_all = lax.all_gather(g_piece, everyone, axis=0).reshape(shape)
        x_all = lax.all_gather(x_piece, everyone, axis=0).reshape(shape)
        own_rows.append(lax.dynamic_index_in_dim(x_all, e_index, 0, False))
        own_dy.append(lax.dynamic_index_in_dim(g_all, e_index, 0, False))
        out_part, dx_part, dgate, *weight_grads = moe_call(
            jnp.full((1,), chunk * chunk_rows, jnp.int32),
            all_lengths,
            x_all,
            g_all,
            info[:, at],
            wgu,
            wd,
            n_local,
            weight_grads,
        )
        flat = (n_expert * n_tensor, chunk_rows, slice_width)
        back_parts.append(lax.psum_scatter(dx_part.reshape(flat), everyone, scatter_dimension=0))
        moe_parts.append(lax.psum_scatter(out_part.reshape(flat), everyone, scatter_dimension=0))
        dgate_parts.append(dgate)
        chain = (back_parts[-1], moe_parts[-1], own_rows[-1], own_dy[-1], weight_grads)
    grad_w_gate, grad_w_up, grad_w_down = weight_grads
    moe_slice = jnp.concatenate(moe_parts, axis=0).astype(jnp.float32)
    back_slice = jnp.concatenate(back_parts, axis=0).astype(jnp.float32)
    output = (valid_rows * (hidden + moe_slice)).astype(jnp.bfloat16)

    def side_by_side(parts):
        rows = jnp.concatenate(parts, axis=1)
        return rows.transpose(1, 0, 2).reshape(tok_rows, model_width)

    rows_full = side_by_side(own_rows).astype(jnp.float32)
    d_out_full = side_by_side(own_dy).astype(jnp.float32) * valid_rows
    d_gates = jnp.concatenate(dgate_parts, axis=1)[:, :, :n_local].transpose(0, 2, 1)
    d_gates = lax.all_to_all(d_gates, "expert", split_axis=0, concat_axis=0, tiled=True)
    d_gates = lax.psum(d_gates.reshape(n_experts, tok_rows), "tensor").T
    d_probs = d_gates * chosen
    d_logits = (
        router_probs * (d_probs - jnp.sum(router_probs * d_probs, axis=-1, keepdims=True))
    ).astype(jnp.bfloat16)
    scaled_logits = (d_logits.astype(jnp.float32) * scale_h).astype(jnp.bfloat16)
    router_grad = cross_dot(moe_rows, scaled_logits)
    back_slice = back_slice + dot_transposed(scaled_logits, router_slice)
    back_full = lax.all_gather(back_slice.astype(jnp.bfloat16), "tensor", axis=1, tiled=True)
    back_full = back_full.astype(jnp.float32)
    projection = jnp.mean(back_full * rows_full, axis=-1, keepdims=True) * scale_h
    h_term = projection * scale_h
    d_hidden = d_out_full + g_moe * back_full - rows_full / g_moe * h_term
    d_attn = d_hidden.astype(jnp.bfloat16)
    d_out_slice = cotangent.astype(jnp.float32) * valid_rows
    d_hidden_slice = d_out_slice + g_moe_slice * back_slice - hidden * h_term
    grad_g_moe = jnp.sum(back_slice * hidden, axis=0)
    grad_w_out = cross_dot(heads_out, d_attn)
    d_heads = dot_transposed(d_attn, w_out).astype(jnp.bfloat16).reshape(head_shape)
    d_query_parts = []
    block_number = 0
    d_keys = jnp.zeros((SLOT, heads_here, HD), jnp.float32)
    d_value_sum = jnp.zeros((SLOT, heads_here, HD), jnp.float32)
    for block_start in range(0, SLOT, block_rows):
        block_end = block_start + block_rows
        query_block = query_heads[block_start:block_end]
        key_prefix = key_heads[:block_end]
        value_prefix = value_heads[:block_end]
        scores, allowed = block_scores(query_block, key_prefix, block_start, lengths[0], factor)
        probs = jnp.where(allowed, jnp.exp(scores - log_totals[block_number]), 0.0)
        block_number += 1
        d_block = d_heads[block_start:block_end]
        d_probs_att = jnp.einsum(
            "qhd,khd->hqk", d_block, value_prefix, preferred_element_type=jnp.float32
        )
        spread = jnp.sum(probs * d_probs_att, axis=-1, keepdims=True)
        d_scores = (factor * probs * (d_probs_att - spread)).astype(jnp.bfloat16)
        d_query_parts.append(
            jnp.einsum("hqk,khd->qhd", d_scores, key_prefix, preferred_element_type=jnp.float32)
        )
        d_keys = d_keys.at[:block_end].add(
            jnp.einsum("hqk,qhd->khd", d_scores, query_block, preferred_element_type=jnp.float32)
        )
        d_value_sum = d_value_sum.at[:block_end].add(
            jnp.einsum(
                "hqk,qhd->khd", probs.astype(jnp.bfloat16), d_block, preferred_element_type=jnp.float32
            )
        )
    d_query = jnp.concatenate(d_query_parts, axis=0)
    d_values = d_value_sum.reshape(tok_rows, heads_here * HD).astype(jnp.bfloat16)
    d_q_norm = unrotate(d_query, cosine, sine_table).reshape(tok_rows, heads_here * HD)
    d_k_norm = unrotate(d_keys, cosine, sine_table).reshape(tok_rows, heads_here * HD)
    q_sum, k_sum = lax.psum(
        (jnp.sum(d_q_norm * g_query * q_raw, axis=1), jnp.sum(d_k_norm * g_key * k_raw, axis=1)),
        "tensor",
    )
    grad_g_query = jnp.sum(d_q_norm * q_raw * scale_q, axis=0)
    grad_g_key = jnp.sum(d_k_norm * k_raw * scale_k, axis=0)
    d_q_raw = (
        scale_q * g_query * d_q_norm - q_raw * scale_q**3 * (q_sum / model_width)[:, None]
    ).astype(jnp.bfloat16)
    d_k_raw = (
        scale_k * g_key * d_k_norm - k_raw * scale_k**3 * (k_sum / model_width)[:, None]
    ).astype(jnp.bfloat16)
    grad_w_query = cross_dot(normed, d_q_raw)
    grad_w_key = cross_dot(normed, d_k_raw)
    grad_w_value = cross_dot(normed, d_values)
    d_normed_part = (
        dot_transposed(d_q_raw, w_query)
        + dot_transposed(d_k_raw, w_key)
        + dot_transposed(d_values, w_value)
    )
    column_sums = jnp.sum(
        d_q_raw.astype(jnp.float32) * q_raw
        + d_k_raw.astype(jnp.float32) * k_raw
        + d_values.astype(jnp.float32) * values.astype(jnp.float32),
        axis=1,
    )
    x_mean = (lax.psum(column_sums, "tensor") / model_width)[:, None]
    d_normed = lax.psum_scatter(
        d_normed_part.astype(jnp.bfloat16), "tensor", scatter_dimension=1, tiled=True
    ).astype(jnp.float32)
    x_hat = block_input.astype(jnp.float32) * scale_x
    grad_g_attn = jnp.sum(d_normed * x_hat, axis=0)
    grad_input = (
        d_hidden_slice + scale_x * (d_normed * own_columns(g_attn) - x_hat * x_mean)
    ).astype(jnp.bfloat16)

    def summed(grad):
        return lax.psum(grad.astype(jnp.bfloat16), "expert").astype(jnp.float32)

    small = jnp.concatenate(
        [router_grad.T, grad_g_moe[None], grad_g_attn[None], grad_g_query[None], grad_g_key[None]],
        axis=0,
    )
    small = lax.psum(small, "expert")
    shared = lax.all_gather(small[: n_experts + 2], "tensor", axis=1, tiled=True)
    return (
        output,
        grad_input,
        shared[n_experts + 1],
        summed(grad_w_query),
        summed(grad_w_key),
        summed(grad_w_value),
        small[n_experts + 2],
        small[n_experts + 3],
        summed(grad_w_out),
        shared[n_experts],
        shared[:n_experts].T,
        grad_w_gate,
        grad_w_up,
        grad_w_down,
    )


def solution(mesh):
    placed = (
        P("expert", "tensor"),
        P("expert", "tensor"),
        P("expert"),
        P("expert", None),
        P(),
        P(None, "tensor"),
        P(None, "tensor"),
        P(None, "tensor"),
        P("tensor"),
        P("tensor"),
        P("tensor", None),
        P(),
        P(),
        P("expert", None, "tensor"),
        P("expert", None, "tensor"),
        P("expert", "tensor", None),
    )
    return jax.shard_map(
        shards,
        mesh=mesh,
        in_specs=placed,
        out_specs=(
            P("expert", "tensor"),
            P("expert", "tensor"),
            P(),
            P(None, "tensor"),
            P(None, "tensor"),
            P(None, "tensor"),
            P("tensor"),
            P("tensor"),
            P("tensor", None),
            P(),
            P(),
            P("expert", None, "tensor"),
            P("expert", None, "tensor"),
            P("expert", "tensor", None),
        ),
        check_vma=False,
    )
```

time: 3370 us -> 1910 us (0.57)
  waiting for transfers between devices: 2360 us -> 1350 us
  local copies, waits for them, and re-layouts: 436 us -> 86.4 us
  matrix products: 319 us -> 81.4 us
  Pallas kernels: 0 us -> 143 us
  blocking collectives: 63.9 us -> 128 us
  other arithmetic: 143 us -> 87.1 us
    all_to_all x4 -> x0, waiting for transfers between devices: 1530 us -> none  [the longest x1 770 us: shards(): lax.all_to_all(d_send, 'expert', split_axis=0, concat_axis=0, tiled=True)]
    gather x6 -> x0, local copies, waits for them, and re-layouts: 323 us -> none  [the longest x1 71.6 us: shards(): dy_padded[token_of_slot].astype(jnp.float32)]
    all_gather x3 -> x4, waiting for transfers between devices: 71.3 us -> 391 us  [the longest x1 196 us: shards(): x_all = lax.all_gather(x_piece, everyone, axis=0).reshape(shape)]
    dot_general x13 -> x4, matrix products: 243 us -> 9.47 us  [the longest x2 4.7 us: shards(): jnp.einsum('hqk,khd->qhd', weights, value_heads[:block_end], preferred_el...]
    reduce_scatter x2 -> x4, waiting for transfers between devices: 474 us -> 688 us  [the longest x1 355 us: shards(): lax.psum_scatter(dx_part.reshape(flat), everyone, scatter_dimension=0)]
    pallas_call x0 -> x1, Pallas kernels: none -> 143 us  [moe_call(): pl.pallas_call(functools.partial(moe_body, resume), out_shape=(jax.ShapeD...]
    all_gather x0 -> x2, blocking collectives: none -> 40.1 us  [the longest x1 34.5 us: shards(): lax.all_gather(jnp.concatenate([gates, scale_h], axis=1).T, 'expert', axi...]
    convert_element_type x0 -> x4, local copies, waits for them, and re-layouts: none -> 36.3 us  [the longest x2 18.3 us: shards(): d_out_full = side_by_side(own_dy).astype(jnp.float32) * valid_rows]
  transfers between devices with their start and end apart: 12 -> 11, of which waited for: 9 -> 10; matrix products, arithmetic and copies ran while one was open for 17% -> 9% of each run, Pallas kernels for 0% -> 0%
where the time goes in v1:
time: 1910 us; the launch traced here: 1890 us
  waiting for transfers between devices  1350 us (71%)
  Pallas kernels  143 us (7%)
  blocking collectives  128 us (7%)
  other arithmetic  87.1 us (5%)
  local copies, waits for them, and re-layouts  86.4 us (5%)
  matrix products  81.4 us (4%)
    reduce_scatter x1, waiting for transfers between devices, shards(): lax.psum_scatter(dx_part.reshape(flat), everyone, scatter_dimension=0)  355 us
    reduce_scatter x1, waiting for transfers between devices, shards(): lax.psum_scatter(out_part.reshape(flat), everyone, scatter_dimension=0)  233 us
    psum x1, waiting for transfers between devices, summed(): return lax.psum(grad.astype(jnp.bfloat16), 'expert').astype(jnp.float32)  223 us
    all_gather x1, waiting for transfers between devices, shards(): x_all = lax.all_gather(x_piece, everyone, axis=0).reshape(shape)  196 us
    all_gather x1, waiting for transfers between devices, shards(): g_all = lax.all_gather(g_piece, everyone, axis=0).reshape(shape)  161 us
    pallas_call x1, Pallas kernels, moe_call(): pl.pallas_call(functools.partial(moe_body, resume), out_shape=(jax.ShapeD...  143 us
    reduce_scatter x1, waiting for transfers between devices, shards(): lax.psum_scatter(d_normed_part.astype(jnp.bfloat16), 'tensor', scatter_di...  55.1 us
    reduce_scatter x1, waiting for transfers between devices, shards(): lax.psum_scatter(attn_part, 'tensor', scatter_dimension=1, tiled=True)  44.7 us
  transfers between devices with their start and end apart: 11, of which 10 were waited for; matrix products, arithmetic and copies ran while one was open for 9% of the time, Pallas kernels for 0%

profile of v1, /device:TPU:0, one launch (start us, length us, event | category | flops | bytes accessed | tf_op | source)
XLA Modules:
  0.0 1888.7 jit_solution(800952206641903184)
XLA Ops:
  12.0 34.8 %all-gather.9.cloned.1.call-done = bf16[1024,2048]{1,0:T(8,128)(2,1)} async-done(((bf16[1024,512]{1,0:T(8,128)(2,1)}), bf16[1024,2048]{1,0:T(8,128)(2,1)}) %all-gather.9.cloned.1.call-update) | async-done | bytes 4194320 | tf_op jit(solution)/shard_map/all_gather | solution.py:267
  46.8 3.2 fusion
  50.2 3.9 multiply_reduce_fusion.5
  54.1 3.9 multiply_reduce_fusion.4
  58.1 6.4 all-reduce.4
  68.4 3.2 copy.163
  71.6 3.2 copy.164
  84.4 5.5 convolution_convert_fusion.6
  102.3 3.2 fusion.54
  106.6 4.4 convolution_convert_fusion
  111.9 44.7 %reduce-scatter.5.cloned.1.call-done = bf16[1024,512]{1,0:T(8,128)(2,1)} async-done(((bf16[1024,2048]{1,0:T(8,128)(2,1)}), bf16[1024,512]{1,0:T(8,128)(2,1)}) %reduce-scatter.5.cloned.1.call-update) | async-done | bytes 1048592 | tf_op jit(solution)/shard_map/reduce_scatter | solution.py:313
  162.4 11.9 all-reduce.2.lens
  179.2 12.5 all-reduce.10.cloned.1.call-done
  195.1 34.5 %all-gather.3 = f32[8,17,1024]{2,1,0:T(8,128)S(1)} all-gather(f32[1,17,1024]{2,1,0:T(8,128)S(1)} %maximum_bitcast_fusion), channel_id=4, replica_groups=mesh['expert'=8,'tensor'=4] {'expert'}, dimensions={0}, use_global_device_ids=true | all-gather | bytes 626688 | tf_op jit(solution)/shard_map/all_gather | solution.py:332
  232.6 160.6 %all-gather.15.cloned.1.call-done = bf16[32768,512]{1,0:T(8,128)(2,1)} async-done(((bf16[1024,512]{1,0:T(8,128)(2,1)}), bf16[32768,512]{1,0:T(8,128)(2,1)}) %all-gather.15.cloned.1.call-update) | async-done | bytes 33554448 | tf_op jit(solution)/shard_map/all_gather | solution.py:354
  393.3 195.6 %all-gather.13.cloned.1.call-done = bf16[32768,512]{1,0:T(8,128)(2,1)} async-done(((bf16[1024,512]{1,0:T(8,128)(2,1)}), bf16[32768,512]{1,0:T(8,128)(2,1)}) %all-gather.13.cloned.1.call-update) | async-done | bytes 33554448 | tf_op jit(solution)/shard_map/all_gather | solution.py:355
  589.5 142.5 %experts.1 = (bf16[8,4,1024,512]{3,2,1,0:T(8,128)(2,1)}, bf16[8,4,1024,512]{3,2,1,0:T(8,128)(2,1)}, f32[8,1024,8]{2,1,0:T(8,128)}, f32[2,2048,256]{2,1,0:T(8,128...) custom-call(s32[1]{0:T(128)} %constant.166.clone.1.starts, s32[8]{0:T(128)} %all-reduce.2.lens, ...), custom_call_target="tpu_custom_call" | custom-call | tf_op jit(solution)/shard_map/experts/pallas_call | solution.py:189
  732.0 4.5 slice_bitcast_fusion
  739.3 10.4 all_to_all.5
  751.2 27.5 %all-reduce.12.cloned.1.call-done = f32[1024,16]{0,1:T(8,128)} async-done(((f32[1024,16]{0,1:T(8,128)}), f32[1024,16]{0,1:T(8,128)}) %all-reduce.12.cloned.1.call-update) | async-done | bytes 65552 | tf_op jit(solution)/shard_map/psum | solution.py:387
  780.5 354.9 %reduce-scatter.9.cloned.1.call-done = bf16[1,1024,512]{2,1,0:T(8,128)(2,1)} async-done(((bf16[32,1024,512]{2,1,0:T(8,128)(2,1)}), bf16[1,1024,512]{2,1,0:T(8,128)(2,1)}) %reduce-scatter.9.cloned.1.call-update) | async-done | bytes 1048592 | tf_op jit(solution)/shard_map/reduce_scatter | solution.py:370
  1135.4 3.3 fusion.101
  1139.6 6.7 convert_bitcast_fusion
  1146.3 8.8 copy.127
  1155.1 9.5 copy.128
  1164.6 6.7 convert_bitcast_fusion.1
  1171.3 8.8 copy.125
  1180.1 9.2 copy.126
  1189.3 5.8 fusion.3
  1197.7 5.4 fusion.6
  1212.9 3.3 multiply_reduce_fusion
  1229.8 4.2 pad_maximum_fusion.2
  1241.1 12.4 all-reduce.3
  1253.6 3.5 fusion.49
  1257.2 5.7 fusion.28
  1270.7 6.5 add_convert_fusion
  1277.5 6.4 convolution_convert_fusion.1
  1283.9 4.2 convolution_convert_fusion.3
  1288.1 4.2 convolution_convert_fusion.4
  1292.3 4.2 convolution_convert_fusion.2
  1298.0 6.8 psum.90
  1304.8 233.4 %reduce-scatter.7.cloned.1.call-done = bf16[1,1024,512]{2,1,0:T(8,128)(2,1)} async-done(((bf16[32,1024,512]{2,1,0:T(8,128)(2,1)}), bf16[1,1024,512]{2,1,0:T(8,128)(2,1)}) %reduce-scatter.7.cloned.1.call-update) | async-done | bytes 1048592 | tf_op jit(solution)/shard_map/reduce_scatter | solution.py:371
  1538.2 55.1 %reduce-scatter.11.cloned.1.call-done = bf16[1024,512]{1,0:T(8,128)(2,1)} async-done(((bf16[1024,2048]{1,0:T(8,128)(2,1)}), bf16[1024,512]{1,0:T(8,128)(2,1)}) %reduce-scatter.11.cloned.1.call-update) | async-done | bytes 1048592 | tf_op jit(solution)/shard_map/reduce_scatter | solution.py:466
  1593.3 5.0 fusion.25
  1598.4 40.4 %psum.91 = f32[20,512]{1,0:T(8,128)S(1)} all-reduce(f32[20,512]{1,0:T(8,128)S(1)} %concatenate.54), channel_id=1, replica_groups=mesh['expert'=8,'tensor'=4] {'expert'}, use_global_device_ids=true, to_apply=%region_33.34 | all-reduce | flops 10240 | bytes 81920 | tf_op jit(solution)/shard_map/psum | solution.py:482
  1638.7 5.6 all_gather.39
  1646.2 223.5 %all-reduce.14.cloned.1.call-done = (bf16[2048,512]{1,0:T(8,128)(2,1)}, bf16[2048,512]{1,0:T(8,128)(2,1)}, bf16[2048,512]{1,0:T(8,128)(2,1)}, bf16[512,2048]{1,0:T(8,128)(2,1)}) async-done(((bf16[2048,512]{1,0:T(8,128)(2,1)}, bf16[2048,512]{1,0:T(8,128)(2,1)}, bf16[2048,512]{1,0:T(8,128)(2,1)}, bf16[512,2048]{1,0:T(8,128)(2,1)}), (bf16[2048,512]{1,0:T(8,128)(2,1)}, bf16[2048,512]{1,0:T(8,128)(2,1)}, ...) | async-done | bytes 8388624 | tf_op jit(solution)/shard_map/psum | solution.py:476
  1869.7 4.3 convert_element_type.222
  (278 shorter events, 108.2 us)
Async XLA Ops:
  7.2 42.8 %copy-start = (bf16[2048,512]{1,0:T(8,128)(2,1)S(1)}, bf16[2048,512]{1,0:T(8,128)(2,1)}, u32[]{:S(2)}) copy-start(bf16[2048,512]{1,0:T(8,128)(2,1)} %param.33) | copy-start | bytes 6291460
  7.2 42.8 %copy-start.75 = (f32[2048]{0:T(1024)S(1)}, f32[2048]{0:T(1024)}, u32[]{:S(2)}) copy-start(f32[2048]{0:T(1024)} %param.32) | copy-start | bytes 24580
  7.2 39.6 %all-gather.9.cloned.1.call-start = ((), (), s32[]{:S(2)}) async-start(), calls=%async_computation.5 | async-start | bytes 5242880 | tf_op jit(solution)/shard_map/all_gather | solution.py:267
  7.9 148.7 %reduce-scatter.5.cloned.1.call-start = ((), (), s32[]{:S(2)}) async-start(), calls=%async_computation.6 | async-start | bytes 5242880 | tf_op jit(solution)/shard_map/reduce_scatter | solution.py:313
  9.2 92.2 %copy-start.18 = (pred[512,1024]{1,0:T(8,128)(4,1)}, pred[512,1024]{1,0:T(8,128)(4,1)S(1)}, u32[]{:S(2)}) copy-start(pred[512,1024]{1,0:T(8,128)(4,1)S(1)} %fusion.44) | copy-start | bytes 1572868
  12.0 78.0 %copy-start.35 = (f32[1024,64]{1,0:T(8,128)}, f32[1024,64]{1,0:T(8,128)S(1)}, u32[]{:S(2)}) copy-start(f32[1024,64]{1,0:T(8,128)S(1)} %get-tuple-element.143) | copy-start | bytes 786436
  50.2 34.1 %copy-start.70 = (f32[1024]{0:T(1024)}, f32[1024]{0:T(1024)S(1)}, u32[]{:S(2)}) copy-start(f32[1024]{0:T(1024)S(1)} %add_rsqrt_fusion.2) | copy-start | bytes 12292
  54.1 11.0 copy-start.65
  65.1 9.6 copy-start.58
  68.4 6.3 copy-start.63
  84.4 5.6 copy-start.27
  84.4 5.6 copy-start.37
  89.9 11.5 copy-start.28
  111.0 47.7 %copy-start.69 = (bf16[2048,16]{0,1:T(8,128)(2,1)S(1)}, bf16[2048,16]{0,1:T(8,128)(2,1)}, u32[]{:S(2)}) copy-start(bf16[2048,16]{0,1:T(8,128)(2,1)} %param.40) | copy-start | bytes 196612
  111.1 50.0 %copy-start.81 = (u32[32]{0:T(128)S(1)}, u32[32]{0:T(128)}, u32[]{:S(2)}) copy-start(u32[32]{0:T(128)} %constant.186) | copy-start | bytes 388
  111.1 63.3 %copy-start.62 = (s32[1024,8]{0,1:T(8,128)S(1)}, s32[1024,8]{0,1:T(8,128)}, u32[]{:S(2)}) copy-start(s32[1024,8]{0,1:T(8,128)} %param.31) | copy-start | bytes 98308
  111.1 80.6 %all-reduce.10.cloned.1.call-start = ((), (), s32[]{:S(2)}) async-start(), calls=%async_computation.7 | async-start | bytes 196608 | tf_op jit(solution)/shard_map/psum | solution.py:325
  111.9 65.0 %copy-start.67 = (f32[512]{0:T(512)}, f32[512]{0:T(512)S(1)}, u32[]{:S(2)}) copy-start(f32[512]{0:T(512)S(1)} %dynamic_slice.19) | copy-start | bytes 6148
  159.8 233.5 %all-gather.15.cloned.1.call-start = ((), (), s32[]{:S(2)}) async-start(), calls=%async_computation.14 | async-start | bytes 34603008 | tf_op jit(solution)/shard_map/all_gather | solution.py:354
  160.4 428.5 %all-gather.13.cloned.1.call-start = ((), (), s32[]{:S(2)}) async-start(), calls=%async_computation.13 | async-start | bytes 34603008 | tf_op jit(solution)/shard_map/all_gather | solution.py:355
  161.0 617.7 %all-reduce.12.cloned.1.call-start = ((), (), s32[]{:S(2)}) async-start(), calls=%async_computation.10 | async-start | bytes 131072 | tf_op jit(solution)/shard_map/psum | solution.py:387
  750.4 385.0 %reduce-scatter.9.cloned.1.call-start = ((), (), s32[]{:S(2)}) async-start(), calls=%async_computation.9 | async-start | bytes 34603008 | tf_op jit(solution)/shard_map/reduce_scatter | solution.py:370
  750.5 28.2 %copy-start.52 = (f32[1024,17]{0,1:T(8,128)S(1)}, f32[1024,17]{0,1:T(8,128)}, u32[]{:S(2)}) copy-start(f32[1024,17]{0,1:T(8,128)} %all-reduce.10.cloned.1.call-done) | copy-start | bytes 208900
  751.2 438.1 %all-gather.11.cloned.1.call-start = ((), (), s32[]{:S(2)}) async-start(), calls=%async_computation.11 | async-start | bytes 5242880 | tf_op jit(solution)/shard_map/all_gather | solution.py:395
  1138.8 399.4 %reduce-scatter.7.cloned.1.call-start = ((), (), s32[]{:S(2)}) async-start(), calls=%async_computation.8 | async-start | bytes 34603008 | tf_op jit(solution)/shard_map/reduce_scatter | solution.py:371
  1139.5 453.8 %reduce-scatter.11.cloned.1.call-start = ((), (), s32[]{:S(2)}) async-start(), calls=%async_computation.12 | async-start | bytes 5242880 | tf_op jit(solution)/shard_map/reduce_scatter | solution.py:466
  1189.3 5.9 copy-start.74
  1189.3 7.2 copy-start.2
  1189.3 8.4 copy-start.13
  1205.6 7.2 copy-start.49
  1229.8 7.1 copy-start.59
  1229.8 7.1 copy-start.64
  1234.0 5.9 copy-start.61
  1234.0 5.9 copy-start.66
  1241.1 16.0 copy-start.50
  1257.1 5.8 copy-start.6
  1257.1 5.8 copy-start.7
  1257.1 5.8 copy-start.8
  1257.1 5.9 copy-start.10
  1257.2 6.2 copy-start.30
  1257.2 6.2 copy-start.72
  1257.2 6.2 copy-start.73
  1277.2 6.7 copy-start.56
  1277.2 6.7 copy-start.71
  1277.2 6.7 copy-start.76
  1277.2 592.5 %all-reduce.14.cloned.1.call-start = ((), (), s32[]{:S(2)}) async-start(), calls=%async_computation.15 | async-start | bytes 16777216 | tf_op jit(solution)/shard_map/psum | solution.py:476
  1277.5 6.4 copy-start.42
  1296.5 296.9 %copy-start.68 = (f32[512]{0:T(512)S(1)}, f32[512]{0:T(512)}, u32[]{:S(2)}) copy-start(f32[512]{0:T(512)} %copy-done.67) | copy-start | bytes 6148
  (47 other events, 146.9 us)
Sparse Core Ops, SparseCore 0:
  9.6 37.1 all-gather.8
  111.2 45.4 reduce-scatter.4
  159.9 31.7 all-reduce.9
  194.4 198.8 all-gather.14
  396.5 192.3 all-gather.12
  750.6 28.1 all-reduce.11
  781.0 354.3 reduce-scatter.8
  1138.9 42.1 all-gather.10
  1183.4 354.7 reduce-scatter.6
  1541.1 52.1 reduce-scatter.10
  1598.5 271.1 all-reduce.13
